TPU v7x, 256 devices: a whole 4x4x8 slice. The times are simulated.
256 devices in a mesh: dp: 32 (over y, x, core), expert: 8 (over z).
Axes of the slice: x: 4, y: 4, z: 8, core: 2. Of those that a mesh axis runs over, the one named last changes fastest.
Arguments:
- tokens: bfloat16 [4096, 2048], P('dp'), may hold values from -6 to 6
- route_expert: int32 [4096, 4], P('dp'), may hold values from 0 to 31, all different within a row; in each aligned block of 128 rows (0 to 127, 128 to 255, ...) at most 32 rows name the same one
- route_weight: float32 [4096, 4], P('dp'), may hold values from 0.1 to 1
- gate_weight: bfloat16 [32, 1408, 2048], P('dp', 'expert'), may hold values from -0.125 to 0.125
- up_weight: bfloat16 [32, 1408, 2048], P('dp', 'expert'), may hold values from -0.125 to 0.125
- down_weight: bfloat16 [32, 1408, 2048], P('dp', 'expert'), may hold values from -0.15625 to 0.15625
- gate_scale: float32 [32, 1408], P('dp', 'expert'), may hold values from 0.5 to 2
- up_scale: float32 [32, 1408], P('dp', 'expert'), may hold values from 0.5 to 2
- down_scale: float32 [32, 2048], replicated, may hold values from 0.5 to 2
- cotangent: bfloat16 [4096, 2048], P('dp', 'expert'), may hold values from -6 to 6
Outputs:
- mixed: bfloat16 [4096, 2048], P('dp', 'expert')
- token_grad: bfloat16 [4096, 2048], P('dp', 'expert')
- route_grad: float32 [4096, 4], P('dp')
- gate_grad: float32 [32, 1408, 2048], P('dp', 'expert')
- up_grad: float32 [32, 1408, 2048], P('dp', 'expert')
- down_grad: float32 [32, 1408, 2048], P('dp', 'expert')
Inputs may be any that keep to these rules, and one draw needn't show every extreme that they name: `route_expert`: each row names 4 different experts. Among the 128 rows of one aligned block (the tokens of one index of dp) no expert is named by more than 32 rows, and in some block one expert is named by exactly 32 rows.
All inputs are finite; a program needn't handle non-finite values.
Results may differ from a plain program's by a relative error of at most 0.0058.
Values may be sent and summed in bfloat16 or wider, within the bound.
No kernel may reach another device: no remote copies, remote signals or barrier semaphores. Data moves between devices by JAX's collectives and lax.ppermute only.
A program may use at most 128 MiB of HBM per device.

v0:
```python
import jax
import jax.numpy as jnp
from jax import lax
from jax.sharding import PartitionSpec as P


def local(
    tokens,
    route_expert,
    route_weight,
    gate_weight,
    up_weight,
    down_weight,
    gate_scale,
    up_scale,
    down_scale,
    cotangent,
):
    owners = lax.axis_size("dp")
    tok_rows, width = tokens.shape
    choose = route_expert.shape[1]
    capacity = 2 * tok_rows * choose // owners
    slots = owners * capacity
    assigned = tok_rows * choose
    col_share = width // lax.axis_size("expert")
    col_start = lax.axis_index("expert") * col_share
    flat_expert = route_expert.reshape(-1)
    one_hot = (flat_expert[:, None] == jnp.arange(owners, dtype=jnp.int32)[None, :]).astype(
        jnp.int32
    )
    ranks = jnp.sum((jnp.cumsum(one_hot, axis=0) - 1) * one_hot, axis=1)
    slot_index = flat_expert * capacity + ranks
    slot_token = (
        jnp.zeros((slots,), jnp.int32)
        .at[slot_index]
        .set(jnp.arange(assigned, dtype=jnp.int32) // choose)
    )
    filled = jnp.zeros((slots,), jnp.bool_).at[slot_index].set(True)
    slot_weight = jnp.zeros((slots,), jnp.float32).at[slot_index].set(route_weight.reshape(-1))
    outgoing = jnp.where(
        filled[:, None], jnp.take(tokens, slot_token, axis=0), jnp.zeros((), tokens.dtype)
    )
    arrived = lax.all_to_all(
        outgoing.reshape(owners, capacity, width), "dp", split_axis=0, concat_axis=0, tiled=True
    ).reshape(slots, width)
    gate_local = gate_weight[0]
    up_local = up_weight[0]
    down_local = down_weight[0]
    gate_pre = (
        lax.dot_general(
            arrived, gate_local, (((1,), (1,)), ((), ())), preferred_element_type=jnp.float32
        )
        * gate_scale[0][None, :]
    )
    up_pre = (
        lax.dot_general(
            arrived, up_local, (((1,), (1,)), ((), ())), preferred_element_type=jnp.float32
        )
        * up_scale[0][None, :]
    )
    sigmoid_gate = jax.nn.sigmoid(gate_pre)
    silu_gate = gate_pre * sigmoid_gate
    hidden = (silu_gate * up_pre).astype(jnp.bfloat16)
    summed = lax.psum_scatter(
        lax.dot_general(
            down_local, hidden, (((0,), (1,)), ((), ())), preferred_element_type=jnp.float32
        ),
        "expert",
        scatter_dimension=0,
        tiled=True,
    )
    owner_scale = lax.dynamic_slice(down_scale, (lax.axis_index("dp"), col_start), (1, col_share))[
        0
    ]
    out_cols = (summed * owner_scale[:, None]).astype(jnp.bfloat16)
    returned = lax.all_to_all(
        out_cols.reshape(col_share, owners, capacity), "dp", split_axis=1, concat_axis=1, tiled=True
    ).reshape(col_share, slots)
    picked = (
        jnp.take(returned, slot_index, axis=1)
        .reshape(col_share, tok_rows, choose)
        .astype(jnp.float32)
    )
    mixed = jnp.sum(picked * route_weight[None, :, :], axis=2).T.astype(jnp.bfloat16)
    cot_cols = cotangent.T.astype(jnp.float32)
    route_part = jnp.sum(picked * cot_cols[:, :, None], axis=0)
    route_grad = lax.psum(route_part, "expert")
    slot_scale = jnp.repeat(down_scale, capacity, axis=0)
    full_cot = lax.all_gather(cotangent, "expert", axis=1, tiled=True)
    cot_slots = jnp.take(full_cot, slot_token, axis=0).astype(jnp.float32)
    weighted = (cot_slots * slot_weight[:, None] * slot_scale).astype(jnp.bfloat16)
    out_grad = lax.all_to_all(
        weighted.reshape(owners, capacity, width), "dp", split_axis=0, concat_axis=0, tiled=True
    ).reshape(slots, width)
    hidden_grad = lax.dot_general(
        out_grad, down_local, (((1,), (1,)), ((), ())), preferred_element_type=jnp.float32
    )
    gate_in = (
        hidden_grad
        * up_pre
        * sigmoid_gate
        * (1.0 + gate_pre * (1.0 - sigmoid_gate))
        * gate_scale[0][None, :]
    ).astype(jnp.bfloat16)
    up_in = (hidden_grad * silu_gate * up_scale[0][None, :]).astype(jnp.bfloat16)
    down_grad = lax.dot_general(
        hidden, out_grad, (((0,), (0,)), ((), ())), preferred_element_type=jnp.float32
    )
    gate_grad = lax.dot_general(
        gate_in, arrived, (((0,), (0,)), ((), ())), preferred_element_type=jnp.float32
    )
    up_grad = lax.dot_general(
        up_in, arrived, (((0,), (0,)), ((), ())), preferred_element_type=jnp.float32
    )
    first = lax.dot_general(
        gate_local, gate_in, (((0,), (1,)), ((), ())), preferred_element_type=jnp.float32
    )
    second = lax.dot_general(
        up_local, up_in, (((0,), (1,)), ((), ())), preferred_element_type=jnp.float32
    )
    input_cols = lax.psum_scatter(first + second, "expert", scatter_dimension=0, tiled=True)
    input_home = lax.all_to_all(
        input_cols.reshape(col_share, owners, capacity),
        "dp",
        split_axis=1,
        concat_axis=1,
        tiled=True,
    ).reshape(col_share, slots)
    token_grad = jnp.sum(
        jnp.take(input_home, slot_index, axis=1).reshape(col_share, tok_rows, choose), axis=2
    ).T.astype(jnp.bfloat16)
    return (mixed, token_grad, route_grad, gate_grad[None], up_grad[None], down_grad[None])


def solution(mesh):
    return jax.shard_map(
        local,
        mesh=mesh,
        in_specs=(
            P("dp", None),
            P("dp", None),
            P("dp", None),
            P("dp", "expert", None),
            P("dp", "expert", None),
            P("dp", "expert", None),
            P("dp", "expert"),
            P("dp", "expert"),
            P(),
            P("dp", "expert"),
        ),
        out_specs=(
            P("dp", "expert"),
            P("dp", "expert"),
            P("dp", None),
            P("dp", "expert", None),
            P("dp", "expert", None),
            P("dp", "expert", None),
        ),
        check_vma=False,
    )
```

profile of v0, /device:TPU:2, one launch (start us, length us, event | category | flops | bytes accessed | tf_op | source)
XLA Modules:
  0.0 436.8 jit_solution(8157642740581195982)
XLA Ops:
  10.0 2.4 scatter_custom_fusion.1
  13.3 29.3 %all_gather.3 = bf16[128,2048]{1,0:T(8,128)(2,1)S(1)} all-gather(bf16[128,256]{1,0:T(8,128)(2,1)} %param.21), channel_id=1, replica_groups=mesh['dp'=32,'expert'=8] {'expert'}, dimensions={1}, use_global_device_ids=true | all-gather | bytes 589824 | tf_op jit(solution)/shard_map/all_gather | solution.py:89
  45.1 6.0 %gather_fusion.3 = bf16[1024,2048]{1,0:T(8,128)(2,1)} fusion(bf16[128,2048]{1,0:T(8,128)(2,1)S(1)} %all_gather.3, s32[1024]{0:T(1024)S(1)} %fusion.13), kind=kCustom, calls=%fused_computation.1.clone | custom fusion | bytes 8392704 | tf_op jit(solution)/shard_map/jit(_take)/gather | solution.py:90
  51.2 4.5 %fusion = bf16[1024,2048]{1,0:T(8,128)(2,1)} fusion(bf16[1024,2048]{1,0:T(8,128)(2,1)} %gather_fusion.3, f32[32,2048]{1,0:T(8,128)S(1)} %copy-done.7, f32[1024]{0:T(1024)S(1)} %scatter_custom_fusion.2, pred[1024]{0:T(1024)(128)(4,1)S(1)} %compare_and_fusion.1), kind=kLoop, calls=%fused_computation.8 | loop fusion | flops 10485760 | bytes 8655872 | tf_op jit(solution)/shard_map/convert_element_type | solution.py:91
  55.6 7.8 %all-to-all-start.2 = ((bf16[32,32,2048]{2,1,0:T(8,128)(2,1)}), bf16[32,32,2048]{2,1,0:T(8,128)(2,1)}, u32[]{:S(2)}, u32[]{:S(2)}) async-start(bf16[32,32,2048]{2,1,0:T(8,128)(2,1)} %bitcast.93), calls=%async_computation.3 | async-start | bytes 8388608 | tf_op jit(solution)/shard_map/all_to_all | solution.py:92
  63.4 6.0 %gather_fusion.2 = bf16[1024,2048]{1,0:T(8,128)(2,1)} fusion(bf16[128,2048]{1,0:T(8,128)(2,1)S(1)} %copy-done.1, s32[1024]{0:T(1024)S(1)} %fusion.13), kind=kCustom, calls=%fused_computation.clone | custom fusion | bytes 8392704 | tf_op jit(solution)/shard_map/jit(_take)/gather | solution.py:41
  69.5 2.4 scatter_custom_fusion
  71.9 4.0 select_select_fusion
  75.9 38.9 %all-to-all-done.2 = bf16[32,32,2048]{2,1,0:T(8,128)(2,1)} async-done(((bf16[32,32,2048]{2,1,0:T(8,128)(2,1)}), bf16[32,32,2048]{2,1,0:T(8,128)(2,1)}, u32[]{:S(2)}, u32[]{:S(2)}) %all-to-all-start.2) | async-done | bytes 4194336 | tf_op jit(solution)/shard_map/all_to_all | solution.py:92
  114.9 7.4 %all-to-all-start = ((bf16[32,32,2048]{2,1,0:T(8,128)(2,1)}), bf16[32,32,2048]{2,1,0:T(8,128)(2,1)}, u32[]{:S(2)}, u32[]{:S(2)}) async-start(bf16[32,32,2048]{2,1,0:T(8,128)(2,1)} %bitcast.92), calls=%async_computation | async-start | bytes 8388608 | tf_op jit(solution)/shard_map/all_to_all | solution.py:43
  122.5 4.6 %fusion.1 = f32[1024,176]{0,1:T(8,128)} fusion(bf16[1024,2048]{1,0:T(8,128)(2,1)} %bitcast.18, bf16[1,176,2048]{2,1,0:T(8,128)(2,1)S(1)} %copy-done.5), kind=kOutput, calls=%fused_computation.18 | convolution fusion | flops 738197504 | bytes 5636096 | tf_op jit(solution)/shard_map/dot_general | solution.py:95
  127.1 46.7 %all-to-all-done = bf16[32,32,2048]{2,1,0:T(8,128)(2,1)} async-done(((bf16[32,32,2048]{2,1,0:T(8,128)(2,1)}), bf16[32,32,2048]{2,1,0:T(8,128)(2,1)}, u32[]{:S(2)}, u32[]{:S(2)}) %all-to-all-start) | async-done | bytes 4194336 | tf_op jit(solution)/shard_map/all_to_all | solution.py:43
  173.8 3.8 convolution_multiply_fusion.1
  177.6 4.0 multiply_convert_fusion.3
  182.4 4.5 %convolution_bitcast_fusion = f32[2048,1024]{0,1:T(8,128)} fusion(bf16[1024,176]{0,1:T(8,128)(2,1)S(1)} %get-tuple-element.15, bf16[1,176,2048]{2,1,0:T(8,128)(2,1)S(1)} %copy-done.5), kind=kOutput, calls=%fused_computation.10 | convolution fusion | flops 738197504 | bytes 9469952 | tf_op jit(solution)/shard_map/dot_general | solution.py:65
  188.3 4.5 %add_bitcast_fusion = f32[2048,1024]{0,1:T(8,128)} fusion(f32[1024,2048]{1,0:T(8,128)S(1)} %fusion.6, bf16[1024,176]{0,1:T(8,128)(2,1)S(1)} %get-tuple-element.17, bf16[1,176,2048]{2,1,0:T(8,128)(2,1)S(1)} %copy-done), kind=kOutput, calls=%fused_computation.9 | convolution fusion | flops 740294656 | bytes 17858560 | tf_op jit(solution)/shard_map/dot_general | solution.py:118
  193.0 85.6 %reduce-scatter.3.cloned.1.call-done = f32[256,1024]{0,1:T(8,128)} async-done(((f32[2048,1024]{0,1:T(8,128)}), f32[256,1024]{0,1:T(8,128)}) %reduce-scatter.3.cloned.1.call-update) | async-done | bytes 1048592 | tf_op jit(solution)/shard_map/reduce_scatter | solution.py:64
  280.7 7.4 %all-to-all-start.1 = ((bf16[256,32,32]{0,2,1:T(8,128)(2,1)}), bf16[256,32,32]{0,2,1:T(8,128)(2,1)S(1)}, u32[]{:S(2)}, u32[]{:S(2)}) async-start(bf16[256,32,32]{0,2,1:T(8,128)(2,1)} %bitcast.12), calls=%async_computation.2 | async-start | bytes 1048576 | tf_op jit(solution)/shard_map/all_to_all | solution.py:76
  288.6 86.1 %reduce-scatter.5.cloned.1.call-done = f32[256,1024]{0,1:T(8,128)} async-done(((f32[2048,1024]{0,1:T(8,128)}), f32[256,1024]{0,1:T(8,128)}) %reduce-scatter.5.cloned.1.call-update) | async-done | bytes 1048592 | tf_op jit(solution)/shard_map/reduce_scatter | solution.py:121
  374.7 7.4 %all-to-all-start.3 = ((f32[256,32,32]{0,2,1:T(8,128)}), f32[256,32,32]{0,2,1:T(8,128)S(1)}, u32[]{:S(2)}, u32[]{:S(2)}) async-start(f32[256,32,32]{0,2,1:T(8,128)} %bitcast.97), calls=%async_computation.5 | async-start | bytes 2097152 | tf_op jit(solution)/shard_map/all_to_all | solution.py:122
  382.2 4.3 convolution_bitcast_fusion.1
  386.5 4.3 convolution_bitcast_fusion.3
  390.8 4.2 convolution_bitcast_fusion.2
  397.4 28.7 %psum.7 = f32[128,4]{1,0:T(8,128)S(1)} all-reduce(f32[128,4]{1,0:T(8,128)S(1)} %reduce_sum.48), channel_id=1, replica_groups=mesh['dp'=32,'expert'=8] {'expert'}, use_global_device_ids=true, to_apply=%region_11.13 | all-reduce | flops 512 | bytes 4096 | tf_op jit(solution)/shard_map/psum | solution.py:87
  (67 shorter events, 17.3 us)
Async XLA Ops:
  7.2 170.4 %copy-start = (bf16[1,176,2048]{2,1,0:T(8,128)(2,1)S(1)}, bf16[1,176,2048]{2,1,0:T(8,128)(2,1)}, u32[]{:S(2)}) copy-start(bf16[1,176,2048]{2,1,0:T(8,128)(2,1)} %param.16) | copy-start | bytes 2162692
  45.1 6.0 %copy-start.7 = (f32[32,2048]{1,0:T(8,128)S(1)}, f32[32,2048]{1,0:T(8,128)}, u32[]{:S(2)}) copy-start(f32[32,2048]{1,0:T(8,128)} %param.20) | copy-start | bytes 786436
  55.6 7.8 %copy-start.1 = (bf16[128,2048]{1,0:T(8,128)(2,1)S(1)}, bf16[128,2048]{1,0:T(8,128)(2,1)}, u32[]{:S(2)}) copy-start(bf16[128,2048]{1,0:T(8,128)(2,1)} %param.12) | copy-start | bytes 1572868
  55.6 59.2 %all-to-all-start.2 = ((bf16[32,32,2048]{2,1,0:T(8,128)(2,1)}), bf16[32,32,2048]{2,1,0:T(8,128)(2,1)}, u32[]{:S(2)}, u32[]{:S(2)}) async-start(bf16[32,32,2048]{2,1,0:T(8,128)(2,1)} %bitcast.93), calls=%async_computation.3 | async-start | bytes 8388608 | tf_op jit(solution)/shard_map/all_to_all | solution.py:92
  114.9 7.7 %copy-start.5 = (bf16[1,176,2048]{2,1,0:T(8,128)(2,1)S(1)}, bf16[1,176,2048]{2,1,0:T(8,128)(2,1)}, u32[]{:S(2)}) copy-start(bf16[1,176,2048]{2,1,0:T(8,128)(2,1)} %param.17) | copy-start | bytes 2162692
  114.9 58.9 %all-to-all-start = ((bf16[32,32,2048]{2,1,0:T(8,128)(2,1)}), bf16[32,32,2048]{2,1,0:T(8,128)(2,1)}, u32[]{:S(2)}, u32[]{:S(2)}) async-start(bf16[32,32,2048]{2,1,0:T(8,128)(2,1)} %bitcast.92), calls=%async_computation | async-start | bytes 8388608 | tf_op jit(solution)/shard_map/all_to_all | solution.py:43
  122.3 51.5 %copy-start.6 = (bf16[1,176,2048]{2,1,0:T(8,128)(2,1)S(1)}, bf16[1,176,2048]{2,1,0:T(8,128)(2,1)}, u32[]{:S(2)}) copy-start(bf16[1,176,2048]{2,1,0:T(8,128)(2,1)} %param.15) | copy-start | bytes 2162692
  122.3 51.5 %copy-start.9 = (f32[1,176]{1,0:T(1,128)S(1)}, f32[1,176]{1,0:T(1,128)}, u32[]{:S(2)}) copy-start(f32[1,176]{1,0:T(1,128)} %param.18) | copy-start | bytes 2116
  122.3 156.3 %reduce-scatter.3.cloned.1.call-start = ((), (), s32[]{:S(2)}) async-start(), calls=%async_computation.6 | async-start | bytes 9437184 | tf_op jit(solution)/shard_map/reduce_scatter | solution.py:64
  127.1 50.5 %copy-start.10 = (f32[1,176]{1,0:T(1,128)S(1)}, f32[1,176]{1,0:T(1,128)}, u32[]{:S(2)}) copy-start(f32[1,176]{1,0:T(1,128)} %param.19) | copy-start | bytes 2116
  173.8 3.8 copy-start.11
  181.7 0.7 copy-start.2
  181.7 6.6 %copy-start.3 = (bf16[1024,176]{0,1:T(8,128)(2,1)}, bf16[1024,176]{0,1:T(8,128)(2,1)S(1)}, u32[]{:S(2)}) copy-start(bf16[1024,176]{0,1:T(8,128)(2,1)S(1)} %get-tuple-element.17) | copy-start | bytes 1081348
  186.9 187.8 %reduce-scatter.5.cloned.1.call-start = ((), (), s32[]{:S(2)}) async-start(), calls=%async_computation.7 | async-start | bytes 9437184 | tf_op jit(solution)/shard_map/reduce_scatter | solution.py:121
  192.8 95.5 %copy-start.8 = (bf16[128,256]{1,0:T(8,128)(2,1)S(1)}, bf16[128,256]{1,0:T(8,128)(2,1)}, u32[]{:S(2)}) copy-start(bf16[128,256]{1,0:T(8,128)(2,1)} %param.21) | copy-start | bytes 196612
  280.7 94.0 %all-to-all-start.1 = ((bf16[256,32,32]{0,2,1:T(8,128)(2,1)}), bf16[256,32,32]{0,2,1:T(8,128)(2,1)S(1)}, u32[]{:S(2)}, u32[]{:S(2)}) async-start(bf16[256,32,32]{0,2,1:T(8,128)(2,1)} %bitcast.12), calls=%async_computation.2 | async-start | bytes 1048576 | tf_op jit(solution)/shard_map/all_to_all | solution.py:76
  374.7 52.0 %all-to-all-start.3 = ((f32[256,32,32]{0,2,1:T(8,128)}), f32[256,32,32]{0,2,1:T(8,128)S(1)}, u32[]{:S(2)}, u32[]{:S(2)}) async-start(f32[256,32,32]{0,2,1:T(8,128)} %bitcast.97), calls=%async_computation.5 | async-start | bytes 2097152 | tf_op jit(solution)/shard_map/all_to_all | solution.py:122
  386.5 4.3 copy-start.4
Sparse Core Ops, SparseCore 0:
  187.0 91.5 reduce-scatter.2
  281.1 93.5 reduce-scatter.4
where the time goes:
time: 437 us
  waiting for transfers between devices  257 us (59%)
  blocking collectives  58 us (13%)
  matrix products  35.5 us (8%)
  starting transfers between devices  30.3 us (7%)
  local copies, waits for them, and re-layouts  27.5 us (6%)
  between operations  14.4 us (3%)
  other arithmetic  13.6 us (3%)
    reduce_scatter x1, waiting for transfers between devices, local(): lax.psum_scatter(first + second, 'expert', scatter_dimension=0, tiled=True)  86.1 us
    reduce_scatter x1, waiting for transfers between devices, local(): lax.psum_scatter(lax.dot_general(down_local, hidden, (((0,), (1,)), ((),...  85.6 us
    all_to_all x1, waiting for transfers between devices, local(): lax.all_to_all(outgoing.reshape(owners, capacity, width), 'dp', split_axi...  46.7 us
    all_to_all x1, waiting for transfers between devices, local(): lax.all_to_all(weighted.reshape(owners, capacity, width), 'dp', split_axi...  38.9 us
    all_gather x1, blocking collectives, local(): full_cot = lax.all_gather(cotangent, 'expert', axis=1, tiled=True)  29.3 us
    psum x1, blocking collectives, local(): route_grad = lax.psum(route_part, 'expert')  28.7 us
  transfers between devices with their start and end apart: 6, of which 4 were waited for; matrix products, arithmetic and copies ran while one was open for 9% of the time, Pallas kernels for 0%

commit v1 on v0

--- a/solution.py
+++ b/solution.py
@@ -86,7 +86,9 @@
     route_part = jnp.sum(picked * cot_cols[:, :, None], axis=0)
     route_grad = lax.psum(route_part, "expert")
     slot_scale = jnp.repeat(down_scale, capacity, axis=0)
-    full_cot = lax.all_gather(cotangent, "expert", axis=1, tiled=True)
+    full_cot = jnp.concatenate(
+        lax.all_to_all(jnp.stack([cotangent] * lax.axis_size("expert")), "expert", 0, 0), axis=1
+    )
     cot_slots = jnp.take(full_cot, slot_token, axis=0).astype(jnp.float32)
     weighted = (cot_slots * slot_weight[:, None] * slot_scale).astype(jnp.bfloat16)
     out_grad = lax.all_to_all(

time: 437 us -> 419 us (0.959)
  blocking collectives: 58 us -> 28.7 us
  starting transfers between devices: 30.3 us -> 38.8 us
    all_gather x1 -> x0, blocking collectives: 29.3 us -> none  [local(): full_cot = lax.all_gather(cotangent, 'expert', axis=1, tiled=True)]
    all_to_all x1, waiting for transfers between devices: 46.7 us -> 38.2 us  [local(): lax.all_to_all(outgoing.reshape(owners, capacity, width), 'dp', split_axi...]
    all_to_all x0 -> x1, starting transfers between devices: none -> 8.47 us  [local(): lax.all_to_all(jnp.stack([cotangent] * lax.axis_size('expert')), 'expert'...]
    all_to_all x1, waiting for transfers between devices: 38.9 us -> 46.7 us  [local(): lax.all_to_all(weighted.reshape(owners, capacity, width), 'dp', split_axi...]
  transfers between devices with their start and end apart: 6 -> 7, of which waited for: 4 -> 4; matrix products, arithmetic and copies ran while one was open for 9% -> 14% of each run, Pallas kernels for 0% -> 0%
where the time goes in v1:
time: 419 us
  waiting for transfers between devices  259 us (62%)
  starting transfers between devices  38.8 us (9%)
  matrix products  35.5 us (8%)
  blocking collectives  28.7 us (7%)
  local copies, waits for them, and re-layouts  28.6 us (7%)
  between operations  14.4 us (3%)
  other arithmetic  13.6 us (3%)
    reduce_scatter x1, waiting for transfers between devices, local(): lax.psum_scatter(lax.dot_general(down_local, hidden, (((0,), (1,)), ((),...  88.1 us
    reduce_scatter x1, waiting for transfers between devices, local(): lax.psum_scatter(first + second, 'expert', scatter_dimension=0, tiled=True)  86.2 us
    all_to_all x1, waiting for transfers between devices, local(): lax.all_to_all(weighted.reshape(owners, capacity, width), 'dp', split_axi...  46.7 us
    all_to_all x1, waiting for transfers between devices, local(): lax.all_to_all(outgoing.reshape(owners, capacity, width), 'dp', split_axi...  38.2 us
    psum x1, blocking collectives, local(): route_grad = lax.psum(route_part, 'expert')  28.7 us
    all_to_all x1, starting transfers between devices, local(): lax.all_to_all(jnp.stack([cotangent] * lax.axis_size('expert')), 'expert'...  8.47 us
  transfers between devices with their start and end apart: 7, of which 4 were waited for; matrix products, arithmetic and copies ran while one was open for 14% of the time, Pallas kernels for 0%

profile of v1, /device:TPU:2, one launch (start us, length us, event | category | flops | bytes accessed | tf_op | source)
XLA Modules:
  0.0 418.8 jit_solution(3969353077312937151)
XLA Ops:
  9.0 8.5 %all-to-all-start.2 = ((bf16[8,128,256]{2,1,0:T(8,128)(2,1)}), bf16[8,128,256]{2,1,0:T(8,128)(2,1)S(1)}, u32[]{:S(2)}, u32[]{:S(2)}) async-start(bf16[8,128,256]{2,1,0:T(8,128)(2,1)} %stack.2), calls=%async_computation.3 | async-start | bytes 1048576 | tf_op jit(solution)/shard_map/all_to_all | solution.py:90
  20.1 2.4 scatter_custom_fusion.1
  22.6 2.4 scatter_custom_fusion
  25.1 6.0 %gather_fusion.2 = bf16[1024,2048]{1,0:T(8,128)(2,1)} fusion(bf16[128,2048]{1,0:T(8,128)(2,1)S(1)} %copy-done.1, s32[1024]{0:T(1024)S(1)} %fusion.13), kind=kCustom, calls=%fused_computation.clone | custom fusion | bytes 8392704 | tf_op jit(solution)/shard_map/jit(_take)/gather | solution.py:41
  31.1 4.0 select_select_fusion
  35.1 7.8 %all-to-all-start = ((bf16[32,32,2048]{2,1,0:T(8,128)(2,1)}), bf16[32,32,2048]{2,1,0:T(8,128)(2,1)}, u32[]{:S(2)}, u32[]{:S(2)}) async-start(bf16[32,32,2048]{2,1,0:T(8,128)(2,1)} %bitcast.96), calls=%async_computation | async-start | bytes 8388608 | tf_op jit(solution)/shard_map/all_to_all | solution.py:43
  45.7 6.0 %gather_fusion.3 = bf16[1024,2048]{1,0:T(8,128)(2,1)} fusion(bf16[128,2048]{1,0:T(8,128)(2,1)S(1)} %bitcast.94, s32[1024]{0:T(1024)S(1)} %fusion.13), kind=kCustom, calls=%fused_computation.1.clone | custom fusion | bytes 8392704 | tf_op jit(solution)/shard_map/jit(_take)/gather | solution.py:92
  51.7 4.5 %fusion = bf16[1024,2048]{1,0:T(8,128)(2,1)} fusion(bf16[1024,2048]{1,0:T(8,128)(2,1)} %gather_fusion.3, f32[32,2048]{1,0:T(8,128)S(1)} %copy-done.7, f32[1024]{0:T(1024)S(1)} %scatter_custom_fusion.2, pred[1024]{0:T(1024)(128)(4,1)S(1)} %compare_and_fusion.1), kind=kLoop, calls=%fused_computation.8 | loop fusion | flops 10485760 | bytes 8655872 | tf_op jit(solution)/shard_map/convert_element_type | solution.py:93
  56.2 38.2 %all-to-all-done = bf16[32,32,2048]{2,1,0:T(8,128)(2,1)} async-done(((bf16[32,32,2048]{2,1,0:T(8,128)(2,1)}), bf16[32,32,2048]{2,1,0:T(8,128)(2,1)}, u32[]{:S(2)}, u32[]{:S(2)}) %all-to-all-start) | async-done | bytes 4194336 | tf_op jit(solution)/shard_map/all_to_all | solution.py:43
  94.4 7.4 %all-to-all-start.3 = ((bf16[32,32,2048]{2,1,0:T(8,128)(2,1)}), bf16[32,32,2048]{2,1,0:T(8,128)(2,1)}, u32[]{:S(2)}, u32[]{:S(2)}) async-start(bf16[32,32,2048]{2,1,0:T(8,128)(2,1)} %bitcast.97), calls=%async_computation.4 | async-start | bytes 8388608 | tf_op jit(solution)/shard_map/all_to_all | solution.py:94
  102.1 4.6 %convolution_multiply_fusion.1 = f32[1024,176]{0,1:T(8,128)} fusion(bf16[1024,2048]{1,0:T(8,128)(2,1)} %bitcast.4, bf16[1,176,2048]{2,1,0:T(8,128)(2,1)S(1)} %copy-done.6, f32[176]{0:T(256)S(1)} %bitcast.111), kind=kOutput, calls=%fused_computation.16 | convolution fusion | flops 738377728 | bytes 5636800 | tf_op jit(solution)/shard_map/dot_general | solution.py:50
  106.6 46.7 %all-to-all-done.3 = bf16[32,32,2048]{2,1,0:T(8,128)(2,1)} async-done(((bf16[32,32,2048]{2,1,0:T(8,128)(2,1)}), bf16[32,32,2048]{2,1,0:T(8,128)(2,1)}, u32[]{:S(2)}, u32[]{:S(2)}) %all-to-all-start.3) | async-done | bytes 4194336 | tf_op jit(solution)/shard_map/all_to_all | solution.py:94
  153.3 3.8 fusion.1
  157.1 4.0 multiply_convert_fusion.3
  161.9 4.5 %convolution_bitcast_fusion = f32[2048,1024]{0,1:T(8,128)} fusion(bf16[1024,176]{0,1:T(8,128)(2,1)S(1)} %get-tuple-element.21, bf16[1,176,2048]{2,1,0:T(8,128)(2,1)S(1)} %copy-done.5), kind=kOutput, calls=%fused_computation.10 | convolution fusion | flops 738197504 | bytes 9469952 | tf_op jit(solution)/shard_map/dot_general | solution.py:65
  167.8 4.5 %add_bitcast_fusion = f32[2048,1024]{0,1:T(8,128)} fusion(f32[1024,2048]{1,0:T(8,128)S(1)} %fusion.6, bf16[1024,176]{0,1:T(8,128)(2,1)S(1)} %get-tuple-element.23, bf16[1,176,2048]{2,1,0:T(8,128)(2,1)S(1)} %copy-done), kind=kOutput, calls=%fused_computation.9 | convolution fusion | flops 740294656 | bytes 17858560 | tf_op jit(solution)/shard_map/dot_general | solution.py:120
  172.5 88.1 %reduce-scatter.3.cloned.1.call-done = f32[256,1024]{0,1:T(8,128)} async-done(((f32[2048,1024]{0,1:T(8,128)}), f32[256,1024]{0,1:T(8,128)}) %reduce-scatter.3.cloned.1.call-update) | async-done | bytes 1048592 | tf_op jit(solution)/shard_map/reduce_scatter | solution.py:64
  262.7 7.4 %all-to-all-start.1 = ((bf16[256,32,32]{0,2,1:T(8,128)(2,1)}), bf16[256,32,32]{0,2,1:T(8,128)(2,1)S(1)}, u32[]{:S(2)}, u32[]{:S(2)}) async-start(bf16[256,32,32]{0,2,1:T(8,128)(2,1)} %bitcast.12), calls=%async_computation.2 | async-start | bytes 1048576 | tf_op jit(solution)/shard_map/all_to_all | solution.py:76
  270.6 86.2 %reduce-scatter.5.cloned.1.call-done = f32[256,1024]{0,1:T(8,128)} async-done(((f32[2048,1024]{0,1:T(8,128)}), f32[256,1024]{0,1:T(8,128)}) %reduce-scatter.5.cloned.1.call-update) | async-done | bytes 1048592 | tf_op jit(solution)/shard_map/reduce_scatter | solution.py:123
  356.8 7.4 %all-to-all-start.4 = ((f32[256,32,32]{0,2,1:T(8,128)}), f32[256,32,32]{0,2,1:T(8,128)S(1)}, u32[]{:S(2)}, u32[]{:S(2)}) async-start(f32[256,32,32]{0,2,1:T(8,128)} %bitcast.102), calls=%async_computation.6 | async-start | bytes 2097152 | tf_op jit(solution)/shard_map/all_to_all | solution.py:124
  364.2 4.3 %convolution_bitcast_fusion.1 = f32[1,176,2048]{2,1,0:T(8,128)} fusion(bf16[1024,176]{0,1:T(8,128)(2,1)} %copy-done.2, bf16[1024,2048]{1,0:T(8,128)(2,1)} %bitcast.19), kind=kOutput, calls=%fused_computation.12 | convolution fusion | flops 738197504 | bytes 5996544 | tf_op jit(solution)/shard_map/dot_general | solution.py:108
  368.5 4.3 %convolution_bitcast_fusion.3 = f32[1,176,2048]{2,1,0:T(8,128)} fusion(bf16[1024,176]{0,1:T(8,128)(2,1)S(1)} %get-tuple-element.22, bf16[1024,2048]{1,0:T(8,128)(2,1)} %bitcast.4), kind=kOutput, calls=%fused_computation.14 | convolution fusion | flops 738197504 | bytes 5996544 | tf_op jit(solution)/shard_map/dot_general | solution.py:111
  372.8 4.2 %convolution_bitcast_fusion.2 = f32[1,176,2048]{2,1,0:T(8,128)} fusion(bf16[1024,176]{0,1:T(8,128)(2,1)S(1)} %copy-done.4, bf16[1024,2048]{1,0:T(8,128)(2,1)} %bitcast.4), kind=kOutput, calls=%fused_computation.13 | convolution fusion | flops 738197504 | bytes 5996544 | tf_op jit(solution)/shard_map/dot_general | solution.py:114
  379.4 28.7 %psum.7 = f32[128,4]{1,0:T(8,128)S(1)} all-reduce(f32[128,4]{1,0:T(8,128)S(1)} %reduce_sum.48), channel_id=1, replica_groups=mesh['dp'=32,'expert'=8] {'expert'}, use_global_device_ids=true, to_apply=%region_11.13 | all-reduce | flops 512 | bytes 4096 | tf_op jit(solution)/shard_map/psum | solution.py:87
  (72 shorter events, 18.4 us)
Async XLA Ops:
  7.2 150.0 %copy-start = (bf16[1,176,2048]{2,1,0:T(8,128)(2,1)S(1)}, bf16[1,176,2048]{2,1,0:T(8,128)(2,1)}, u32[]{:S(2)}) copy-start(bf16[1,176,2048]{2,1,0:T(8,128)(2,1)} %param.16) | copy-start | bytes 2162692
  7.2 17.9 %copy-start.1 = (bf16[128,2048]{1,0:T(8,128)(2,1)S(1)}, bf16[128,2048]{1,0:T(8,128)(2,1)}, u32[]{:S(2)}) copy-start(bf16[128,2048]{1,0:T(8,128)(2,1)} %param.12) | copy-start | bytes 1572868
  9.0 26.2 %all-to-all-start.2 = ((bf16[8,128,256]{2,1,0:T(8,128)(2,1)}), bf16[8,128,256]{2,1,0:T(8,128)(2,1)S(1)}, u32[]{:S(2)}, u32[]{:S(2)}) async-start(bf16[8,128,256]{2,1,0:T(8,128)(2,1)} %stack.2), calls=%async_computation.3 | async-start | bytes 1048576 | tf_op jit(solution)/shard_map/all_to_all | solution.py:90
  35.1 7.8 %copy-start.9 = (f32[128,4]{0,1:T(4,128)S(1)}, f32[128,4]{0,1:T(4,128)}, u32[]{:S(2)}) copy-start(f32[128,4]{0,1:T(4,128)} %param.14) | copy-start | bytes 6148
  35.1 59.2 %all-to-all-start = ((bf16[32,32,2048]{2,1,0:T(8,128)(2,1)}), bf16[32,32,2048]{2,1,0:T(8,128)(2,1)}, u32[]{:S(2)}, u32[]{:S(2)}) async-start(bf16[32,32,2048]{2,1,0:T(8,128)(2,1)} %bitcast.96), calls=%async_computation | async-start | bytes 8388608 | tf_op jit(solution)/shard_map/all_to_all | solution.py:43
  45.7 6.0 %copy-start.7 = (f32[32,2048]{1,0:T(8,128)S(1)}, f32[32,2048]{1,0:T(8,128)}, u32[]{:S(2)}) copy-start(f32[32,2048]{1,0:T(8,128)} %param.20) | copy-start | bytes 786436
  94.4 7.7 %copy-start.6 = (bf16[1,176,2048]{2,1,0:T(8,128)(2,1)S(1)}, bf16[1,176,2048]{2,1,0:T(8,128)(2,1)}, u32[]{:S(2)}) copy-start(bf16[1,176,2048]{2,1,0:T(8,128)(2,1)} %param.15) | copy-start | bytes 2162692
  94.4 7.7 %copy-start.10 = (f32[1,176]{1,0:T(1,128)S(1)}, f32[1,176]{1,0:T(1,128)}, u32[]{:S(2)}) copy-start(f32[1,176]{1,0:T(1,128)} %param.18) | copy-start | bytes 2116
  94.4 58.9 %all-to-all-start.3 = ((bf16[32,32,2048]{2,1,0:T(8,128)(2,1)}), bf16[32,32,2048]{2,1,0:T(8,128)(2,1)}, u32[]{:S(2)}, u32[]{:S(2)}) async-start(bf16[32,32,2048]{2,1,0:T(8,128)(2,1)} %bitcast.97), calls=%async_computation.4 | async-start | bytes 8388608 | tf_op jit(solution)/shard_map/all_to_all | solution.py:94
  101.8 51.5 %copy-start.5 = (bf16[1,176,2048]{2,1,0:T(8,128)(2,1)S(1)}, bf16[1,176,2048]{2,1,0:T(8,128)(2,1)}, u32[]{:S(2)}) copy-start(bf16[1,176,2048]{2,1,0:T(8,128)(2,1)} %param.17) | copy-start | bytes 2162692
  101.8 158.8 %reduce-scatter.3.cloned.1.call-start = ((), (), s32[]{:S(2)}) async-start(), calls=%async_computation.7 | async-start | bytes 9437184 | tf_op jit(solution)/shard_map/reduce_scatter | solution.py:64
  106.6 50.5 %copy-start.11 = (f32[1,176]{1,0:T(1,128)S(1)}, f32[1,176]{1,0:T(1,128)}, u32[]{:S(2)}) copy-start(f32[1,176]{1,0:T(1,128)} %param.19) | copy-start | bytes 2116
  153.3 3.8 copy-start.12
  161.2 0.7 copy-start.2
  161.2 6.6 %copy-start.3 = (bf16[1024,176]{0,1:T(8,128)(2,1)}, bf16[1024,176]{0,1:T(8,128)(2,1)S(1)}, u32[]{:S(2)}) copy-start(bf16[1024,176]{0,1:T(8,128)(2,1)S(1)} %get-tuple-element.23) | copy-start | bytes 1081348
  166.4 190.3 %reduce-scatter.5.cloned.1.call-start = ((), (), s32[]{:S(2)}) async-start(), calls=%async_computation.8 | async-start | bytes 9437184 | tf_op jit(solution)/shard_map/reduce_scatter | solution.py:123
  172.3 98.0 %copy-start.8 = (bf16[128,256]{1,0:T(8,128)(2,1)S(1)}, bf16[128,256]{1,0:T(8,128)(2,1)}, u32[]{:S(2)}) copy-start(bf16[128,256]{1,0:T(8,128)(2,1)} %param.21) | copy-start | bytes 196612
  262.7 94.1 %all-to-all-start.1 = ((bf16[256,32,32]{0,2,1:T(8,128)(2,1)}), bf16[256,32,32]{0,2,1:T(8,128)(2,1)S(1)}, u32[]{:S(2)}, u32[]{:S(2)}) async-start(bf16[256,32,32]{0,2,1:T(8,128)(2,1)} %bitcast.12), calls=%async_computation.2 | async-start | bytes 1048576 | tf_op jit(solution)/shard_map/all_to_all | solution.py:76
  356.8 52.0 %all-to-all-start.4 = ((f32[256,32,32]{0,2,1:T(8,128)}), f32[256,32,32]{0,2,1:T(8,128)S(1)}, u32[]{:S(2)}, u32[]{:S(2)}) async-start(f32[256,32,32]{0,2,1:T(8,128)} %bitcast.102), calls=%async_computation.6 | async-start | bytes 2097152 | tf_op jit(solution)/shard_map/all_to_all | solution.py:124
  368.5 4.3 %copy-start.4 = (bf16[1024,176]{0,1:T(8,128)(2,1)S(1)}, bf16[1024,176]{0,1:T(8,128)(2,1)}, u32[]{:S(2)}) copy-start(bf16[1024,176]{0,1:T(8,128)(2,1)} %copy-done.3) | copy-start | bytes 1081348
Sparse Core Ops, SparseCore 0:
  166.6 93.9 reduce-scatter.2
  263.1 93.5 reduce-scatter.4
